TPU v7x, 256 devices: a whole 4x4x8 slice. The times are simulated.
256 devices in a mesh: patch: 16 (over z_hi, x), wrow: 4 (over z_lo, core), wcol: 4 (over y).
Axes of the slice: x: 4, y: 4, z: 8 (z_hi: 4, z_lo: 2; z = z_hi * 2 + z_lo), core: 2. Of those that a mesh axis runs over, the one named last changes fastest.
Arguments:
- hidden_states: bfloat16 [4, 8192, 1536], P('wrow', ('patch', 'wcol')), may hold values from -6 to 6
- modulation: float32 [4, 3, 1536], P('wrow'), may hold values from -4 to 4
- w_qkv: bfloat16 [1536, 3, 1536], P('wrow', None, 'wcol'), may hold values from -1 to 1
- w_out: bfloat16 [1536, 1536], P('wcol', 'wrow'), may hold values from -0.15625 to 0.15625
- lengths: int32 [4], P('wrow'), may hold values from 1 to 8192, 20480 in all
Outputs:
- updated: bfloat16 [4, 8192, 1536], P('wrow', ('patch', 'wcol'))
Inputs may be any that keep to these rules, and one draw needn't show every extreme that they name: lengths[v] real tokens in video v, padding after them; the longest video fills all 8192 slots.
All inputs are finite; a program needn't handle non-finite values. No bound on the sum of `lengths` on one device may be relied on, other than what follows from the above.
Results may differ from a plain program's by a relative error of at most 0.015.
The roundings to bfloat16 on the way count: a program that leaves them out, or rounds other values in their place, can miss the bound.
Values may be sent and summed in bfloat16 or wider, within the bound.
A program may use at most 64 MiB of HBM per device.

v0:
```python
import jax
import jax.numpy as jnp
from jax import lax
from jax.sharding import PartitionSpec as P

HD = 128


EPSILON = 1e-06
FLOOR = -1e30


def modulated_norm(states, shift, scale):
    values = states.astype(jnp.float32)
    center = jnp.mean(values, axis=-1, keepdims=True)
    spread = jnp.mean(jnp.square(values - center), axis=-1, keepdims=True)
    return ((values - center) * lax.rsqrt(spread + EPSILON) * (1.0 + scale) + shift).astype(
        jnp.bfloat16
    )


def absorb(carry, keys, values, first, queries, limits):
    peak, weight_sum, numer = carry
    videos_here = keys.shape[0]
    count = keys.shape[1]
    heads_here = queries.shape[2]
    head_size = queries.shape[3]
    key_heads = keys.reshape(videos_here, count, heads_here, head_size)
    value_heads = values.reshape(videos_here, count, heads_here, head_size)
    scores = jnp.einsum(
        "vqhd,vkhd->vhqk", queries, key_heads, preferred_element_type=jnp.float32
    ) * head_size ** (-0.5)
    position = first + jnp.arange(count, dtype=jnp.int32)
    valid = (position[None, :] < limits[:, None])[:, None, None, :]
    scores = jnp.where(valid, scores, FLOOR)
    new_peak = jnp.maximum(peak, jnp.max(scores, axis=-1))
    factor = jnp.exp(peak - new_peak)
    probs = jnp.exp(scores - new_peak[..., None]) * valid.astype(jnp.float32)
    weight_sum = weight_sum * factor + jnp.sum(probs, axis=-1)
    numer = numer * factor[..., None] + jnp.einsum(
        "vhqk,vkhd->vhqd",
        probs.astype(jnp.bfloat16),
        value_heads,
        preferred_element_type=jnp.float32,
    )
    return (new_peak, weight_sum, numer)


def body(hidden_states, modulation, w_qkv, w_out, lengths):
    videos_here = hidden_states.shape[0]
    width = hidden_states.shape[2]
    shift = modulation[:, 0][:, None, :]
    scale = modulation[:, 1][:, None, :]
    gate = modulation[:, 2][:, None, :]
    normed = modulated_norm(hidden_states, shift, scale)
    tile_rows = lax.all_gather(normed, "wcol", axis=1, tiled=True)
    tile_len = tile_rows.shape[1]
    local_cols = w_qkv.shape[2]
    flat_rows = tile_rows.reshape(videos_here * tile_len, width)
    piece = lax.all_gather(w_qkv, "wrow", axis=0, tiled=True)
    mixed = jnp.dot(
        flat_rows, piece.reshape(piece.shape[0], 3 * local_cols), preferred_element_type=jnp.float32
    )
    mixed = mixed.reshape(videos_here, tile_len, 3 * local_cols)
    mixed = mixed.astype(jnp.bfloat16).reshape(videos_here, tile_len, 3, local_cols)
    heads_here = local_cols // HD
    queries = mixed[:, :, 0].reshape(videos_here, tile_len, heads_here, HD)
    keys = mixed[:, :, 1]
    values = mixed[:, :, 2]
    start_peak = jnp.full((videos_here, heads_here, tile_len), FLOOR, jnp.float32)
    start_sum = jnp.zeros((videos_here, heads_here, tile_len), jnp.float32)
    start_numer = jnp.zeros((videos_here, heads_here, tile_len, HD), jnp.float32)
    key_piece = lax.all_gather(keys, "patch", axis=1, tiled=True)
    value_piece = lax.all_gather(values, "patch", axis=1, tiled=True)
    count = key_piece.shape[1]
    block_len = 512

    def one_block(index, inner):
        offset = index * block_len
        key_block = lax.dynamic_slice_in_dim(key_piece, offset, block_len, 1)
        value_block = lax.dynamic_slice_in_dim(value_piece, offset, block_len, 1)
        return absorb(inner, key_block, value_block, offset, queries, lengths)

    peak, weight_sum, numer = lax.fori_loop(
        0, count // block_len, one_block, (start_peak, start_sum, start_numer)
    )
    attended = (numer / weight_sum[..., None]).astype(jnp.bfloat16)
    attended = jnp.transpose(attended, (0, 2, 1, 3)).reshape(videos_here * tile_len, local_cols)
    partial_out = jnp.dot(
        attended,
        lax.all_gather(w_out, "wrow", axis=1, tiled=True),
        preferred_element_type=jnp.float32,
    )
    partial_out = partial_out.reshape(videos_here, tile_len, width)
    out_proj = lax.psum_scatter(
        partial_out.astype(jnp.bfloat16), "wcol", scatter_dimension=1, tiled=True
    ).astype(jnp.float32)
    return (hidden_states.astype(jnp.float32) + gate * out_proj).astype(jnp.bfloat16)


def solution(mesh):
    placed = (
        P("wrow", ("patch", "wcol"), None),
        P("wrow", None, None),
        P("wrow", None, "wcol"),
        P("wcol", "wrow"),
        P("wrow"),
    )
    return jax.shard_map(
        body,
        mesh=mesh,
        in_specs=placed,
        out_specs=P("wrow", ("patch", "wcol"), None),
        check_vma=False,
    )
```

profile of v0, /device:TPU:2, one launch (start us, length us, event | category | flops | bytes accessed | tf_op | source)
XLA Modules:
  0.0 490.6 jit_solution(7066353537932086624)
XLA Ops:
  14.8 29.8 %all-gather.8.cloned.1.call-done = bf16[1,512,1536]{2,1,0:T(8,128)(2,1)} async-done(((bf16[1,128,1536]{2,1,0:T(8,128)(2,1)}), bf16[1,512,1536]{2,1,0:T(8,128)(2,1)}) %all-gather.8.cloned.1.call-update) | async-done | bytes 1572880 | tf_op jit(solution)/shard_map/all_gather | solution.py:56
  44.6 45.2 %all-gather.10.cloned.1.call-done = bf16[1536,3,384]{0,2,1:T(8,128)(2,1)} async-done(((bf16[384,3,384]{0,2,1:T(8,128)(2,1)}), bf16[1536,3,384]{0,2,1:T(8,128)(2,1)}) %all-gather.10.cloned.1.call-update) | async-done | bytes 3538960 | tf_op jit(solution)/shard_map/all_gather | solution.py:60
  89.8 4.7 convolution_convert_fusion
  97.7 103.0 %all-gather.14.cloned.1.call-done = bf16[1,8192,1,384]{1,3,2,0:T(8,128)(2,1)} async-done(((bf16[1,512,1,384]{1,3,2,0:T(8,128)(2,1)}), bf16[1,8192,1,384]{1,3,2,0:T(8,128)(2,1)}) %all-gather.14.cloned.1.call-update) | async-done | bytes 6291472 | tf_op jit(solution)/shard_map/all_gather | solution.py:73
  200.7 104.5 %all-gather.16.cloned.1.call-done = bf16[1,8192,1,384]{1,3,2,0:T(8,128)(2,1)} async-done(((bf16[1,512,1,384]{1,3,2,0:T(8,128)(2,1)}), bf16[1,8192,1,384]{1,3,2,0:T(8,128)(2,1)}) %all-gather.16.cloned.1.call-update) | async-done | bytes 6291472 | tf_op jit(solution)/shard_map/all_gather | solution.py:74
  305.2 143.9 %while.18 = (s32[]{:T(128)}, f32[1,3,512]{2,1,0:T(4,128)S(1)}, f32[1,3,512]{2,1,0:T(4,128)}, f32[1,3,512,128]{3,2,1,0:T(8,128)}, s32[1]{0:T(128)}, /*index=5*/bf...) while((s32[]{:T(128)}, f32[1,3,512]{2,1,0:T(4,128)S(1)}, ...), condition=%wide.region_5.6_spmd.clone, body=%wide.region_2.5_spmd.clone.sunk | while | flops 413477376 | bytes 13930823 | solution.py:84
  309.3 3.2 fusion.46
  318.0 3.5 fusion.46
  327.1 3.4 fusion.46
  336.1 3.4 fusion.46
  345.1 3.4 fusion.46
  354.1 3.4 fusion.46
  363.1 3.4 fusion.46
  372.1 3.4 fusion.46
  381.1 3.4 fusion.46
  390.1 3.4 fusion.46
  399.2 3.4 fusion.46
  408.2 3.4 fusion.46
  417.2 3.4 fusion.46
  426.2 3.4 fusion.46
  435.2 3.4 fusion.46
  444.2 3.4 fusion.46
  451.5 3.4 fusion.17
  454.9 27.0 %reduce-scatter.2.cloned.1.call-done = bf16[1,128,1536]{2,1,0:T(8,128)(2,1)} async-done(((bf16[1,512,1536]{2,1,0:T(8,128)(2,1)}), bf16[1,128,1536]{2,1,0:T(8,128)(2,1)}) %reduce-scatter.2.cloned.1.call-update) | async-done | bytes 393232 | tf_op jit(solution)/shard_map/reduce_scatter | solution.py:95
  (305 shorter events, 103.1 us)
Async XLA Ops:
  6.5 38.1 %all-gather.8.cloned.1.call-start = ((), (), s32[]{:S(2)}) async-start(), calls=%async_computation.1 | async-start | bytes 1966080 | tf_op jit(solution)/shard_map/all_gather | solution.py:56
  12.4 77.4 %all-gather.10.cloned.1.call-start = ((), (), s32[]{:S(2)}) async-start(), calls=%async_computation.2 | async-start | bytes 4423680 | tf_op jit(solution)/shard_map/all_gather | solution.py:60
  14.7 186.0 %all-gather.14.cloned.1.call-start = ((), (), s32[]{:S(2)}) async-start(), calls=%async_computation.5 | async-start | bytes 6684672 | tf_op jit(solution)/shard_map/all_gather | solution.py:73
  96.2 209.0 %all-gather.16.cloned.1.call-start = ((), (), s32[]{:S(2)}) async-start(), calls=%async_computation.6 | async-start | bytes 6684672 | tf_op jit(solution)/shard_map/all_gather | solution.py:74
  96.8 354.7 %all-gather.12.cloned.1.call-start = ((), (), s32[]{:S(2)}) async-start(), calls=%async_computation.3 | async-start | bytes 1474560 | tf_op jit(solution)/shard_map/all_gather | solution.py:91
  97.4 384.6 %reduce-scatter.2.cloned.1.call-start = ((), (), s32[]{:S(2)}) async-start(), calls=%async_computation.4 | async-start | bytes 1966080 | tf_op jit(solution)/shard_map/reduce_scatter | solution.py:95
  318.0 3.5 copy-start.3
  318.0 3.5 copy-start.5
  327.0 3.5 copy-start.3
  336.1 3.5 copy-start.3
  345.1 3.5 copy-start.3
  354.1 3.5 copy-start.3
  363.1 3.5 copy-start.3
  372.1 3.5 copy-start.3
  381.1 3.5 copy-start.3
  390.1 3.5 copy-start.3
  399.1 3.5 copy-start.3
  408.1 3.5 copy-start.3
  417.2 3.5 copy-start.3
  426.2 3.5 copy-start.3
  435.2 3.5 copy-start.3
  444.2 3.5 copy-start.3
  450.6 31.3 %copy-start = (bf16[1,128,1536]{2,1,0:T(8,128)(2,1)S(1)}, bf16[1,128,1536]{2,1,0:T(8,128)(2,1)}, u32[]{:S(2)}) copy-start(bf16[1,128,1536]{2,1,0:T(8,128)(2,1)} %param.7) | copy-start | bytes 1179652
  450.6 31.3 %copy-start.6 = (f32[1536]{0:T(1024)S(1)}, f32[1536]{0:T(1024)}, u32[]{:S(2)}) copy-start(f32[1536]{0:T(1024)} %get-tuple-element.182) | copy-start | bytes 18436
  (64 other events, 91.9 us)
Sparse Core Ops, SparseCore 0:
  12.5 32.0 all-gather.7
  46.4 43.3 all-gather.9
  96.3 104.3 all-gather.13
  203.0 102.2 all-gather.15
  306.9 22.7 all-gather.11
  455.0 26.8 reduce-scatter.1
where the time goes:
time: 492 us; the launch traced here: 491 us
  waiting for transfers between devices  311 us (63%)
  matrix products  76 us (15%)
  local copies, waits for them, and re-layouts  45.7 us (9%)
  other arithmetic  43.1 us (9%)
  between operations  13.6 us (3%)
    all_gather x1, waiting for transfers between devices, body(): value_piece = lax.all_gather(values, 'patch', axis=1, tiled=True)  105 us
    all_gather x1, waiting for transfers between devices, body(): key_piece = lax.all_gather(keys, 'patch', axis=1, tiled=True)  103 us
    dot_general x16, matrix products, absorb(): jnp.einsum('vhqk,vkhd->vhqd', probs.astype(jnp.bfloat16), value_heads, pr...  54.9 us
    all_gather x1, waiting for transfers between devices, body(): piece = lax.all_gather(w_qkv, 'wrow', axis=0, tiled=True)  45.2 us
    dynamic_slice x16, local copies, waits for them, and re-layouts, one_block(): value_block = lax.dynamic_slice_in_dim(value_piece, offset, block_len, 1)  30.6 us
    all_gather x1, waiting for transfers between devices, body(): tile_rows = lax.all_gather(normed, 'wcol', axis=1, tiled=True)  29.8 us
    reduce_scatter x1, waiting for transfers between devices, body(): lax.psum_scatter(partial_out.astype(jnp.bfloat16), 'wcol', scatter_dimens...  27 us
    convert_element_type x16, other arithmetic, absorb(): probs = jnp.exp(scores - new_peak[..., None]) * valid.astype(jnp.float32)  19.9 us
  transfers between devices with their start and end apart: 6, of which 5 were waited for; matrix products, arithmetic and copies ran while one was open for 28% of the time, Pallas kernels for 0%

commit v1 on v0

v1 whole, which is shorter than its diff:
```python
import functools
import math

import jax
import jax.numpy as jnp
from jax import lax
from jax.experimental import pallas as pl
from jax.experimental.pallas import tpu as pltpu
from jax.sharding import PartitionSpec as P

HD = 128
HEADS_HERE = 3
TILE = 512
ROWS = 128
WIDTH = 1536
EPSILON = 1e-06
FLOOR = -1e30
SCORE_SCALE = HD**-0.5 * math.log2(math.e)
MESH = pl.DeviceIdType.MESH


def mod(a, n):
    return lax.rem(a + 2 * n, n)


def place():
    patch, wrow, y = lax.axis_index("patch"), lax.axis_index("wrow"), lax.axis_index("wcol")
    return patch // 4, lax.rem(patch, 4), wrow // 2, lax.rem(wrow, 2), y


def device(zh, x, zl, core, y):
    return (zh * 4 + x, zl * 2 + core, y)


def remote(src, dst, send_sem, recv_sem, target):
    return pltpu.make_async_remote_copy(
        src_ref=src,
        dst_ref=dst,
        send_sem=send_sem,
        recv_sem=recv_sem,
        device_id=target,
        device_id_type=MESH,
    )


def meet(targets):
    barrier = pltpu.get_barrier_semaphore()
    for target in targets:
        pl.semaphore_signal(barrier, inc=1, device_id=target, device_id_type=MESH)
    pl.semaphore_wait(barrier, len(targets))


def front_kernel(
    x_ref, mod_ref, w_ref, q_ref, k_ref, vt_ref, rows, weights, w_send, w_recv, y_send, y_recv, own_sem
):
    zh, x, zl, core, y = place()
    wrow = zl * 2 + core
    z = zh * 2 + zl
    up, down = mod(z + 1, 8), mod(z - 1, 8)
    other = 1 - core
    ups = [device(up // 2, x, lax.rem(up, 2), c, y) for c in (core, other)]
    downs = [device(down // 2, x, lax.rem(down, 2), c, y) for c in (core, other)]
    partner = device(zh, x, zl, other, y)
    peers = [device(zh, x, zl, core, mod(y + d, 4)) for d in (1, 2, 3)]
    meet(ups + downs + [partner] + peers)

    depth = w_ref.shape[0]
    half = depth // 2
    first = pl.multiple_of(wrow * depth, depth)
    copies = []
    for i, target in enumerate(ups):
        copies.append(
            remote(
                w_ref.at[pl.ds(half, half)],
                weights.at[pl.ds(first + half, half)],
                w_send.at[i],
                w_recv.at[i],
                target,
            )
        )
    for i, target in enumerate(downs):
        copies.append(
            remote(
                w_ref.at[pl.ds(0, half)],
                weights.at[pl.ds(first, half)],
                w_send.at[2 + i],
                w_recv.at[2 + i],
                target,
            )
        )
    copies.append(
        remote(w_ref, weights.at[pl.ds(first, depth)], w_send.at[4], w_recv.at[4], partner)
    )
    for copy in copies:
        copy.start()
    own = pltpu.make_async_copy(w_ref, weights.at[pl.ds(first, depth)], own_sem)
    own.start()

    values = x_ref[...].astype(jnp.float32)
    center = jnp.mean(values, axis=-1, keepdims=True)
    values = values - center
    spread = jnp.mean(jnp.square(values), axis=-1, keepdims=True)
    normed = values * lax.rsqrt(spread + EPSILON) * (1.0 + mod_ref[1:2]) + mod_ref[0:1]
    rows[y] = normed.astype(jnp.bfloat16)
    sends = []
    for d in (1, 3, 2):
        sends.append(remote(rows.at[y], rows.at[y], y_send.at[d], y_recv.at[d], peers[d - 1]))
    for copy in sends:
        copy.start()

    own.wait()
    for copy in copies:
        copy.wait_recv()
    for copy in sends:
        copy.wait_recv()

    flat = rows[...].reshape(4 * ROWS, WIDTH)
    cols = HEADS_HERE * HD
    part = jnp.dot(flat, weights[:, :cols], preferred_element_type=jnp.float32) * SCORE_SCALE
    for h in range(HEADS_HERE):
        q_ref[h] = part[:, h * HD : (h + 1) * HD].astype(jnp.bfloat16)
    part = jnp.dot(flat, weights[:, cols : 2 * cols], preferred_element_type=jnp.float32)
    for h in range(HEADS_HERE):
        k_ref[h] = part[:, h * HD : (h + 1) * HD].astype(jnp.bfloat16)
    part = jnp.dot(flat, weights[:, 2 * cols :], preferred_element_type=jnp.float32)
    for h in range(HEADS_HERE):
        vt_ref[h] = part[:, h * HD : (h + 1) * HD].T.astype(jnp.bfloat16)
    for copy in copies:
        copy.wait_send()
    for copy in sends:
        copy.wait_send()


def front(states, modulation, weights):
    vmem = pl.BlockSpec(memory_space=pltpu.VMEM)
    return pl.pallas_call(
        front_kernel,
        name="front",
        out_shape=(
            jax.ShapeDtypeStruct((HEADS_HERE, TILE, HD), jnp.bfloat16),
            jax.ShapeDtypeStruct((HEADS_HERE, TILE, HD), jnp.bfloat16),
            jax.ShapeDtypeStruct((HEADS_HERE, HD, TILE), jnp.bfloat16),
        ),
        in_specs=[vmem] * 3,
        out_specs=[vmem] * 3,
        scratch_shapes=[
            pltpu.VMEM((4, ROWS, WIDTH), jnp.bfloat16),
            pltpu.VMEM((WIDTH, 3 * HEADS_HERE * HD), jnp.bfloat16),
            pltpu.SemaphoreType.DMA((5,)),
            pltpu.SemaphoreType.DMA((5,)),
            pltpu.SemaphoreType.DMA((4,)),
            pltpu.SemaphoreType.DMA((4,)),
            pltpu.SemaphoreType.DMA,
        ],
        compiler_params=pltpu.CompilerParams(
            collective_id=0, has_side_effects=True, vmem_limit_bytes=40 << 20
        ),
    )(states, modulation, weights)


ORDER = (
    (0, 0), (0, 1), (0, 3), (1, 0), (0, 2), (3, 0), (1, 1), (1, 3),
    (2, 0), (3, 1), (3, 3), (1, 2), (2, 1), (2, 3), (3, 2), (2, 2),
)


def attend_kernel(
    len_ref, q_in, k_in, vt_in, out_ref,
    q_buf, k_buf, vt_buf, peak_ref, sum_ref, numer_ref, done_buf, att_buf,
    z_send, z_recv, x_send, x_recv, o_send, o_recv, own_sem,
):
    zh, x, zl, core, y = place()
    video = zl * 2 + core
    limit = len_ref[0]

    def head_of(row):
        return mod(row - video - 1, 4)

    head = head_of(zh)
    active = head < HEADS_HERE
    right, left = device(zh, mod(x + 1, 4), zl, core, y), device(zh, mod(x - 1, 4), zl, core, y)
    row_devices = {}
    for dz in range(4):
        for dy in range(4):
            row_devices[dz, dy] = device(mod(zh + dz, 4), x, zl, core, mod(y + dy, 4))
    meet([right, left] + [row_devices[key] for key in row_devices if key != (0, 0)])

    def z_copies(d):
        there = head_of(mod(zh + d, 4))
        there = jnp.minimum(there, HEADS_HERE - 1)
        block = zh * 4 + x
        target = row_devices[d, 0]
        return (
            remote(q_in.at[there], q_buf.at[zh], z_send.at[0, d], z_recv.at[0, d], target),
            remote(k_in.at[there], k_buf.at[block], z_send.at[1, d], z_recv.at[1, d], target),
            remote(vt_in.at[there], vt_buf.at[block], z_send.at[2, d], z_recv.at[2, d], target),
        )

    def sends_to(d):
        return head_of(mod(zh + d, 4)) < HEADS_HERE

    for which in range(3):
        for d in (1, 3, 2):
            @pl.when(sends_to(d))
            def _():
                z_copies(d)[which].start()

    def x_copies(d):
        source = mod(zh - d, 4)
        mine = source * 4 + x
        from_left = source * 4 + mod(x - 1, 4)
        from_right = source * 4 + mod(x + 1, 4)

        def one(buf, block, i, target):
            return remote(buf.at[block], buf.at[block], x_send.at[d, i], x_recv.at[d, i], target)

        return (
            one(k_buf, mine, 0, right),
            one(vt_buf, mine, 1, right),
            one(k_buf, mine, 2, left),
            one(vt_buf, mine, 3, left),
            one(k_buf, from_left, 4, right),
            one(vt_buf, from_right, 5, left),
        )

    def spread(d):
        for copy in x_copies(d)[:4]:
            copy.start()

    def wait_z(d):
        z_copies(d)[1].wait_recv()
        z_copies(d)[2].wait_recv()

    def pass_on(d):
        copies = x_copies(d)
        for copy in copies[:4]:
            copy.wait_recv()
        copies[4].start()
        copies[5].start()

    def wait_far(d):
        copies = x_copies(d)
        copies[4].wait_recv()
        copies[5].wait_recv()

    def out_copy(dz, dy):
        tile = mod(zh + dz, 4)
        part = mod(y + dy, 4)
        first = pl.multiple_of(tile * TILE + part * ROWS, ROWS)
        column = pl.multiple_of((y * HEADS_HERE + jnp.minimum(head, HEADS_HERE - 1)) * HD, HD)
        i = dz * 4 + dy
        src = done_buf.at[pl.ds(first, ROWS)]
        dst = att_buf.at[:, pl.ds(column, HD)]
        if i == 0:
            return pltpu.make_async_copy(src, dst, o_send.at[0])
        return remote(src, dst, o_send.at[i], o_recv.at[i], row_devices[dz, dy])

    @pl.when(active)
    def _():
        block = zh * 4 + x
        mine = jnp.minimum(head, HEADS_HERE - 1)
        own = (
            pltpu.make_async_copy(q_in.at[mine], q_buf.at[zh], own_sem.at[0]),
            pltpu.make_async_copy(k_in.at[mine], k_buf.at[block], own_sem.at[1]),
            pltpu.make_async_copy(vt_in.at[mine], vt_buf.at[block], own_sem.at[2]),
        )
        for copy in own:
            copy.start()
        for copy in own:
            copy.wait()
        spread(0)
        peak_ref[...] = jnp.full_like(peak_ref, FLOOR)
        sum_ref[...] = jnp.zeros_like(sum_ref)
        numer_ref[...] = jnp.zeros_like(numer_ref)
        for d in (1, 3, 2):
            z_copies(d)[0].wait_recv()

        def step(i, carry):
            before = {
                1: lambda: pass_on(0),
                3: lambda: (wait_z(1), spread(1)),
                4: lambda: wait_far(0),
                5: lambda: (wait_z(3), spread(3)),
                6: lambda: pass_on(1),
                8: lambda: (wait_z(2), spread(2)),
                9: lambda: pass_on(3),
                11: lambda: wait_far(1),
                12: lambda: pass_on(2),
                14: lambda: wait_far(3),
                15: lambda: wait_far(2),
            }
            for at, act in before.items():
                @pl.when(i == at)
                def _():
                    act()
            back_z, back_x = 0, 0
            for at, (dz, dx) in enumerate(ORDER):
                back_z = jnp.where(i == at, dz, back_z)
                back_x = jnp.where(i == at, dx, back_x)
            block = mod(zh - back_z, 4) * 4 + mod(x - back_x, 4)
            queries = q_buf[...].reshape(4 * TILE, HD)
            scores = lax.dot_general(
                k_buf[block], queries, (((1,), (1,)), ((), ())), preferred_element_type=jnp.float32
            )
            position = block * TILE + lax.broadcasted_iota(jnp.int32, (TILE, 1), 0)
            scores = scores + jnp.where(position < limit, 0.0, FLOOR)
            peak = peak_ref[...]
            new_peak = jnp.maximum(peak, jnp.max(scores, axis=0, keepdims=True))
            factor = jnp.exp2(peak - new_peak)
            probs = jnp.exp2(scores - new_peak).astype(jnp.bfloat16)
            with_ones = jnp.concatenate([vt_buf[block], jnp.ones((16, TILE), jnp.bfloat16)], 0)
            mixed = jnp.dot(with_ones, probs, preferred_element_type=jnp.float32)
            peak_ref[...] = new_peak
            sum_ref[...] = sum_ref[...] * factor + mixed[HD : HD + 1]
            numer_ref[...] = numer_ref[...] * factor + mixed[:HD]
            return carry

        lax.fori_loop(0, 16, step, 0)
        attended = numer_ref[...] / sum_ref[...]
        done_buf[...] = attended.T.astype(jnp.bfloat16)
        for dz in range(4):
            for dy in range(4):
                out_copy(dz, dy).start()
        for d in range(4):
            for copy in x_copies(d):
                copy.wait_send()
        out_copy(0, 0).wait()
        for dz in range(4):
            for dy in range(4):
                if dz + dy > 0:
                    out_copy(dz, dy).wait_send()

    for d in (1, 3, 2):
        @pl.when(sends_to(d))
        def _():
            for copy in z_copies(d):
                copy.wait_send()

    for dz in range(4):
        @pl.when(head_of(mod(zh - dz, 4)) < HEADS_HERE)
        def _():
            for dy in range(4):
                if dz + dy > 0:
                    out_copy(dz, dy).wait_recv()
    out_ref[...] = att_buf[...]


def attend(lengths, q, k, vt):
    vmem = pl.BlockSpec(memory_space=pltpu.VMEM)
    return pl.pallas_call(
        attend_kernel,
        name="attend",
        out_shape=jax.ShapeDtypeStruct((ROWS, WIDTH), jnp.bfloat16),
        in_specs=[pl.BlockSpec(memory_space=pltpu.SMEM)] + [vmem] * 3,
        out_specs=vmem,
        scratch_shapes=[
            pltpu.VMEM((4, TILE, HD), jnp.bfloat16),
            pltpu.VMEM((16, TILE, HD), jnp.bfloat16),
            pltpu.VMEM((16, HD, TILE), jnp.bfloat16),
            pltpu.VMEM((1, 4 * TILE), jnp.float32),
            pltpu.VMEM((1, 4 * TILE), jnp.float32),
            pltpu.VMEM((HD, 4 * TILE), jnp.float32),
            pltpu.VMEM((4 * TILE, HD), jnp.bfloat16),
            pltpu.VMEM((ROWS, WIDTH), jnp.bfloat16),
            pltpu.SemaphoreType.DMA((3, 4)),
            pltpu.SemaphoreType.DMA((3, 4)),
            pltpu.SemaphoreType.DMA((4, 6)),
            pltpu.SemaphoreType.DMA((4, 6)),
            pltpu.SemaphoreType.DMA((16,)),
            pltpu.SemaphoreType.DMA((16,)),
            pltpu.SemaphoreType.DMA((3,)),
        ],
        compiler_params=pltpu.CompilerParams(
            collective_id=1, has_side_effects=True, vmem_limit_bytes=48 << 20
        ),
    )(lengths, q, k, vt)


def body(hidden_states, modulation, w_qkv, w_out, lengths):
    states = hidden_states[0]
    w_full = lax.all_gather(w_out, "wrow", axis=1, tiled=True)
    w_full = lax.all_gather(w_full, "wcol", axis=0, tiled=True)
    q, k, vt = front(states, modulation[0], w_qkv.reshape(w_qkv.shape[0], -1))
    attended = attend(lengths, q, k, vt)
    out_proj = jnp.dot(attended, w_full, preferred_element_type=jnp.float32)
    gate = modulation[0, 2][None]
    return (states.astype(jnp.float32) + gate * out_proj).astype(jnp.bfloat16)[None]


def solution(mesh):
    placed = (
        P("wrow", ("patch", "wcol"), None),
        P("wrow", None, None),
        P("wrow", None, "wcol"),
        P("wcol", "wrow"),
        P("wrow"),
    )
    return jax.shard_map(
        body,
        mesh=mesh,
        in_specs=placed,
        out_specs=P("wrow", ("patch", "wcol"), None),
        check_vma=False,
    )
```

time: 492 us -> 166 us (0.34)
  waiting for transfers between devices: 311 us -> 29.8 us
  Pallas kernels: 0 us -> 113 us
  matrix products: 76 us -> 3.87 us
  other arithmetic: 43.1 us -> 0 us
  local copies, waits for them, and re-layouts: 45.7 us -> 4.8 us
    all_gather x5 -> x2, waiting for transfers between devices: 283 us -> 29.1 us  [the longest x1 29 us: body(): w_full = lax.all_gather(w_out, 'wrow', axis=1, tiled=True)]
    pallas_call x0 -> x2, Pallas kernels: none -> 113 us  [the longest x1 74.8 us: attend(): pl.pallas_call(attend_kernel, name='attend', out_shape=jax.ShapeDtypeStru...]
    dot_general x34 -> x1, matrix products: 76 us -> 3.87 us  [body(): out_proj = jnp.dot(attended, w_full, preferred_element_type=jnp.float32)]
    dynamic_slice x16 -> x0, local copies, waits for them, and re-layouts: 30.6 us -> none  [one_block(): value_block = lax.dynamic_slice_in_dim(value_piece, offset, block_len, 1)]
    reduce_scatter x1 -> x0, waiting for transfers between devices: 27 us -> none  [body(): lax.psum_scatter(partial_out.astype(jnp.bfloat16), 'wcol', scatter_dimens...]
    convert_element_type x19 -> x0, other arithmetic: 24.6 us -> none  [the longest x16 19.9 us: absorb(): probs = jnp.exp(scores - new_peak[..., None]) * valid.astype(jnp.float32)]
    reduce_sum x18 -> x0, other arithmetic: 16.6 us -> none  [the longest x16 14.2 us: absorb(): weight_sum = weight_sum * factor + jnp.sum(probs, axis=-1)]
    while x177 -> x0, local copies, waits for them, and re-layouts: 10.9 us -> none
  transfers between devices with their start and end apart: 6 -> 2, of which waited for: 5 -> 1; matrix products, arithmetic and copies ran while one was open for 28% -> 3% of each run, Pallas kernels for 0% -> 68%
where the time goes in v1:
time: 166 us; the launch traced here: 165 us
  Pallas kernels  113 us (68%)
  waiting for transfers between devices  29.8 us (18%)
  between operations  14.1 us (8%)
  local copies, waits for them, and re-layouts  4.8 us (3%)
  matrix products  3.87 us (2%)
    pallas_call x1, Pallas kernels, attend(): pl.pallas_call(attend_kernel, name='attend', out_shape=jax.ShapeDtypeStru...  74.8 us
    pallas_call x1, Pallas kernels, front(): pl.pallas_call(front_kernel, name='front', out_shape=(jax.ShapeDtypeStruc...  37.8 us
    all_gather x1, waiting for transfers between devices, body(): w_full = lax.all_gather(w_out, 'wrow', axis=1, tiled=True)  29 us
    dot_general x1, matrix products, body(): out_proj = jnp.dot(attended, w_full, preferred_element_type=jnp.float32)  3.87 us
  transfers between devices with their start and end apart: 2, of which 1 were waited for; matrix products, arithmetic and copies ran while one was open for 3% of the time, Pallas kernels for 68%

profile of v1, /device:TPU:2, one launch (start us, length us, event | category | flops | bytes accessed | tf_op | source)
XLA Modules:
  0.0 165.3 jit_solution(12057261439539754670)
XLA Ops:
  6.5 0.0 copy-start
  6.5 0.0 all-gather.3.cloned.1.call-start
  6.5 0.7 all-gather.3.cloned.1.call-update
  7.3 0.0 all-gather.5.cloned.1.call-start
  7.3 29.0 %all-gather.3.cloned.1.call-done = bf16[384,1536]{1,0:T(8,128)(2,1)} async-done(((bf16[384,384]{1,0:T(8,128)(2,1)}), bf16[384,1536]{1,0:T(8,128)(2,1)}) %all-gather.3.cloned.1.call-update) | async-done | bytes 1179664 | tf_op jit(solution)/shard_map/all_gather | solution.py:381
  36.4 0.0 all-gather.5.cloned.1.call-update
  37.0 0.7 copy.11
  37.8 2.5 %copy.7 = bf16[384,3,384]{0,2,1:T(8,128)(2,1)S(1)} copy(bf16[384,3,384]{2,0,1:T(8,128)(2,1)} %param.7) | data formatting | bytes 1769472 | tf_op args[2]
  40.2 0.9 copy.8.w_ref
  41.1 0.0 copy-done
  41.1 37.8 %front.1 = (bf16[3,512,128]{2,1,0:T(8,128)(2,1)S(1)}, bf16[3,512,128]{2,1,0:T(8,128)(2,1)S(1)}, bf16[3,128,512]{2,1,0:T(8,128)(2,1)S(1)}) custom-call(bf16[128,1536]{1,0:T(8,128)(2,1)S(1)} %bitcast.10, f32[3,1536]{1,0:T(4,128)S(1)} %bitcast.11, bf16[384,1152]{1,0:T(8,128)(2,1)S(1)} %copy.8.w_ref), custom_call_target="tpu_custom_call" | custom-call | tf_op jit(solution)/shard_map/front/pallas_call | solution.py:136
  79.0 74.8 %attend.1 = bf16[128,1536]{1,0:T(8,128)(2,1)S(1)} custom-call(s32[1]{0:T(128)S(6)} %copy.12.len_ref, bf16[3,512,128]{2,1,0:T(8,128)(2,1)S(1)} %get-tuple-element.8.q_in, bf16[3,512,128]{2,1,0:T(8,128)(2,1)S(1)} %get-tuple-element.9.k_in, bf16[3,128,512]{2,1,0:T(8,128)(2,1)S(1)} %get-tuple-element.10.vt_in), custom_call_target="tpu_custom_call" | custom-call | tf_op jit(solution)/shard_map/attend/pallas_call | solution.py:350
  153.8 0.7 slice_reduce_fusion
  154.5 0.0 all-gather.5.cloned.1.call-done
  154.6 3.9 %fusion.2 = bf16[1,128,1536]{2,1,0:T(8,128)(2,1)} fusion(bf16[128,1536]{1,0:T(8,128)(2,1)S(1)} %attend.1, bf16[1536,1536]{1,0:T(8,128)(2,1)} %all-gather.5.cloned.1.call-done, f32[1536]{0:T(1024)S(1)} %slice_reduce_fusion, bf16[1,128,1536]{2,1,0:T(8,128)(2,1)S(1)} %copy-done), kind=kOutput, calls=%fused_computation.3 | convolution fusion | flops 604766208 | bytes 5904384 | tf_op jit(solution)/shard_map/dot_general | solution.py:385
Async XLA Ops:
  6.5 34.6 %copy-start = (bf16[1,128,1536]{2,1,0:T(8,128)(2,1)S(1)}, bf16[1,128,1536]{2,1,0:T(8,128)(2,1)}, u32[]{:S(2)}) copy-start(bf16[1,128,1536]{2,1,0:T(8,128)(2,1)} %param.5) | copy-start | bytes 1179652
  6.5 29.8 %all-gather.3.cloned.1.call-start = ((), (), s32[]{:S(2)}) async-start(), calls=%async_computation | async-start | bytes 1474560 | tf_op jit(solution)/shard_map/all_gather | solution.py:381
  7.3 147.3 %all-gather.5.cloned.1.call-start = ((), (), s32[]{:S(2)}) async-start(), calls=%async_computation.1 | async-start | bytes 5898240 | tf_op jit(solution)/shard_map/all_gather | solution.py:382
Sparse Core Ops, SparseCore 0:
  9.2 27.1 all-gather.2
  38.2 65.6 all-gather.4

commit v2 on v0

v2 whole, which is shorter than its diff:
```python
import math

import jax
import jax.numpy as jnp
from jax import lax
from jax.experimental import pallas as pl
from jax.experimental.pallas import tpu as pltpu
from jax.sharding import PartitionSpec as P

HD = 128
HEADS_HERE = 3
TILE = 512
ROWS = 128
WIDTH = 1536
PART = 384
HALF = PART // 2
EPSILON = 1e-06
FLOOR = -1e30
SCORE_SCALE = HD**-0.5 * math.log2(math.e)
MESH = pl.DeviceIdType.MESH

ORDER = (
    (0, 0), (0, 1), (0, 3), (1, 0), (0, 2), (3, 0), (1, 1), (1, 3),
    (2, 0), (3, 1), (3, 3), (1, 2), (2, 1), (2, 3), (3, 2), (2, 2),
)


def mod(a, n):
    return lax.rem(a + 2 * n, n)


def device(zh, x, zl, core, y):
    return (zh * 4 + x, zl * 2 + core, y)


def remote(src, dst, send_sem, recv_sem, target):
    return pltpu.make_async_remote_copy(
        src_ref=src,
        dst_ref=dst,
        send_sem=send_sem,
        recv_sem=recv_sem,
        device_id=target,
        device_id_type=MESH,
    )


def kernel(
    len_ref, x_ref, mod_ref, w_ref, wo_ref, out_ref,
    rows, weights, wo_buf, q_in, k_in, vt_in,
    q_buf, k_buf, vt_buf, peak_ref, sum_ref, numer_ref, done_buf, att_buf,
    w_send, w_recv, a_send, a_recv, b_send, b_recv, r_send, r_recv, y_send, y_recv,
    z_send, z_recv, x_send, x_recv, o_send, o_recv, own_sem,
):
    patch, video, y = lax.axis_index("patch"), lax.axis_index("wrow"), lax.axis_index("wcol")
    zh, x = patch // 4, lax.rem(patch, 4)
    zl, core = video // 2, lax.rem(video, 2)
    z = zh * 2 + zl
    limit = len_ref[0]

    def at(dzh=0, dx=0, dy=0):
        return device(mod(zh + dzh, 4), mod(x + dx, 4), zl, core, mod(y + dy, 4))

    up_z, down_z = mod(z + 1, 8), mod(z - 1, 8)
    up = device(up_z // 2, x, lax.rem(up_z, 2), core, y)
    down = device(down_z // 2, x, lax.rem(down_z, 2), core, y)
    partner = device(zh, x, zl, 1 - core, y)
    right, left = at(dx=1), at(dx=-1)

    barrier = pltpu.get_barrier_semaphore()
    targets = [up, down, partner, right, left]
    targets += [at(dzh=dz, dy=dy) for dz in range(4) for dy in range(4) if dz + dy > 0]
    for target in targets:
        pl.semaphore_signal(barrier, inc=1, device_id=target, device_id_type=MESH)
    pl.semaphore_wait(barrier, len(targets))

    mine_first = pl.multiple_of(video * PART, PART)
    theirs_first = pl.multiple_of(((1 - zl) * 2 + core) * PART, PART)

    def w_copy(i):
        if i == 0:
            src, first, count, target = w_ref.at[:, pl.ds(HALF, HALF)], mine_first + HALF, HALF, up
        elif i == 1:
            src, first, count, target = w_ref.at[:, pl.ds(0, HALF)], mine_first, HALF, down
        elif i == 2:
            src, first, count, target = w_ref, mine_first, PART, partner
        else:
            first, count, target = theirs_first + (HALF if i == 3 else 0), HALF, partner
            src = weights.at[:, pl.ds(first, count)]
        return remote(src, weights.at[:, pl.ds(first, count)], w_send.at[i], w_recv.at[i], target)

    wo_rows = pl.multiple_of(y * PART, PART)

    def a_copy(i):
        first = wo_rows + (HALF if i in (0, 3) else 0)
        count = PART if i == 2 else HALF
        column = mine_first if i < 3 else theirs_first
        target = (up, down, partner, partner, partner)[i]
        src = wo_buf.at[pl.ds(first, count), pl.ds(column, PART)]
        return remote(src, src, a_send.at[i], a_recv.at[i], target)

    def b_copy(d):
        part = wo_buf.at[pl.ds(wo_rows + core * HALF, HALF)]
        return remote(part, part, b_send.at[d], b_recv.at[d], at(dy=d))

    def r_copy(d):
        part = wo_buf.at[pl.ds(mod(y - d, 4) * PART + core * HALF, HALF)]
        return remote(part, part, r_send.at[d], r_recv.at[d], partner)

    def own_w():
        return pltpu.make_async_copy(w_ref, weights.at[:, pl.ds(mine_first, PART)], own_sem.at[3])

    def own_wo():
        return pltpu.make_async_copy(
            wo_ref, wo_buf.at[pl.ds(wo_rows, PART), pl.ds(mine_first, PART)], own_sem.at[4]
        )

    def y_copy(d):
        return remote(rows.at[y], rows.at[y], y_send.at[d], y_recv.at[d], at(dy=d))

    for i in (0, 1, 2):
        w_copy(i).start()
    own_w().start()
    own_wo().start()

    values = x_ref[...].astype(jnp.float32)
    center = jnp.mean(values, axis=-1, keepdims=True)
    values = values - center
    spread = jnp.mean(jnp.square(values), axis=-1, keepdims=True)
    normed = values * lax.rsqrt(spread + EPSILON) * (1.0 + mod_ref[1]) + mod_ref[0]
    rows[y] = normed.astype(jnp.bfloat16)
    for d in (1, 3, 2):
        y_copy(d).start()

    own_wo().wait()
    for i in (0, 1):
        w_copy(i).wait_recv()
        w_copy(3 + i).start()
    for i in (0, 1, 2):
        a_copy(i).start()
    own_w().wait()
    for i in (2, 3, 4):
        w_copy(i).wait_recv()
    for d in (1, 3, 2):
        y_copy(d).wait_recv()

    def head_of(row):
        return mod(row - video - 1, 4)

    head = head_of(zh)
    active = head < HEADS_HERE
    head = jnp.minimum(head, HEADS_HERE - 1)
    own_block = zh * 4 + x
    z_refs = ((q_in, q_buf, zh), (k_in, k_buf, own_block), (vt_in, vt_buf, own_block))

    def z_copy(which, d):
        source, dest, index = z_refs[which]
        there = jnp.minimum(head_of(mod(zh + d, 4)), HEADS_HERE - 1)
        return remote(
            source.at[there], dest.at[index], z_send.at[which, d], z_recv.at[which, d], at(dzh=d)
        )

    def sends_to(d):
        return head_of(mod(zh + d, 4)) < HEADS_HERE

    def own_copy(which):
        source, dest, index = z_refs[which]
        return pltpu.make_async_copy(source.at[head], dest.at[index], own_sem.at[which])

    def hand_out(which):
        @pl.when(active)
        def _():
            own_copy(which).start()

        for d in (1, 3, 2):
            @pl.when(sends_to(d))
            def _():
                z_copy(which, d).start()

    flat = rows[...].reshape(4 * ROWS, WIDTH)
    for which in range(3):
        part = jnp.dot(flat, weights[which], preferred_element_type=jnp.float32)
        if which == 0:
            part = part * SCORE_SCALE
        for h in range(HEADS_HERE):
            one = part[:, h * HD : (h + 1) * HD]
            if which == 2:
                vt_in[h] = one.T.astype(jnp.bfloat16)
            else:
                z_refs[which][0][h] = one.astype(jnp.bfloat16)
        hand_out(which)

    for i in (0, 1):
        a_copy(i).wait_recv()
        a_copy(3 + i).start()

    def x_copy(d, i):
        source = mod(zh - d, 4)
        column = (x, x, x, x, mod(x - 1, 4), mod(x + 1, 4))[i]
        buf = (k_buf, vt_buf, k_buf, vt_buf, k_buf, vt_buf)[i]
        target = (right, right, left, left, right, left)[i]
        block = source * 4 + column
        return remote(buf.at[block], buf.at[block], x_send.at[d, i], x_recv.at[d, i], target)

    def spread_out(d):
        for i in range(4):
            x_copy(d, i).start()

    def wait_z(d):
        z_copy(1, d).wait_recv()
        z_copy(2, d).wait_recv()

    def pass_on(d):
        for i in range(4):
            x_copy(d, i).wait_recv()
        x_copy(d, 4).start()
        x_copy(d, 5).start()

    def wait_far(d):
        x_copy(d, 4).wait_recv()
        x_copy(d, 5).wait_recv()

    def out_copy(dz, dy):
        first = pl.multiple_of(mod(zh + dz, 4) * TILE + mod(y + dy, 4) * ROWS, ROWS)
        column = pl.multiple_of((y * HEADS_HERE + head) * HD, HD)
        i = dz * 4 + dy
        src = done_buf.at[pl.ds(first, ROWS)]
        dst = att_buf.at[:, pl.ds(column, HD)]
        if i == 0:
            return pltpu.make_async_copy(src, dst, o_send.at[0])
        return remote(src, dst, o_send.at[i], o_recv.at[i], at(dzh=dz, dy=dy))

    def start_b():
        for i in (2, 3, 4):
            a_copy(i).wait_recv()
        for d in (1, 3, 2):
            b_copy(d).start()

    def relay_b():
        for d in (1, 3, 2):
            b_copy(d).wait_recv()
            r_copy(d).start()

    @pl.when(active)
    def _():
        for which in range(3):
            own_copy(which).wait()
        spread_out(0)
        peak_ref[...] = jnp.full_like(peak_ref, FLOOR)
        sum_ref[...] = jnp.zeros_like(sum_ref)
        numer_ref[...] = jnp.zeros_like(numer_ref)
        for d in (1, 3, 2):
            z_copy(0, d).wait_recv()

    start_b()

    @pl.when(active)
    def _():
        def step(i, carry):
            before = {
                1: lambda: pass_on(0),
                3: lambda: (wait_z(1), spread_out(1)),
                4: lambda: wait_far(0),
                5: lambda: (wait_z(3), spread_out(3)),
                6: lambda: pass_on(1),
                8: lambda: (wait_z(2), spread_out(2)),
                9: lambda: pass_on(3),
                11: lambda: wait_far(1),
                12: lambda: pass_on(2),
                14: lambda: wait_far(3),
                15: lambda: wait_far(2),
            }
            for when, act in before.items():
                @pl.when(i == when)
                def _():
                    act()
            back_z, back_x = 0, 0
            for when, (dz, dx) in enumerate(ORDER):
                back_z = jnp.where(i == when, dz, back_z)
                back_x = jnp.where(i == when, dx, back_x)
            block = mod(zh - back_z, 4) * 4 + mod(x - back_x, 4)
            queries = q_buf[...].reshape(4 * TILE, HD)
            scores = lax.dot_general(
                k_buf[block], queries, (((1,), (1,)), ((), ())), preferred_element_type=jnp.float32
            )
            position = block * TILE + lax.broadcasted_iota(jnp.int32, (TILE, 1), 0)
            scores = scores + jnp.where(position < limit, 0.0, FLOOR)
            peak = peak_ref[...]
            new_peak = jnp.maximum(peak, jnp.max(scores, axis=0, keepdims=True))
            factor = jnp.exp2(peak - new_peak)
            probs = jnp.exp2(scores - new_peak).astype(jnp.bfloat16)
            with_ones = jnp.concatenate([vt_buf[block], jnp.ones((16, TILE), jnp.bfloat16)], 0)
            mixed = jnp.dot(with_ones, probs, preferred_element_type=jnp.float32)
            peak_ref[...] = new_peak
            sum_ref[...] = sum_ref[...] * factor + mixed[HD : HD + 1]
            numer_ref[...] = numer_ref[...] * factor + mixed[:HD]
            return carry

        lax.fori_loop(0, 16, step, 0)
        attended = numer_ref[...] / sum_ref[...]
        done_buf[...] = attended.T.astype(jnp.bfloat16)
        for dz in range(4):
            for dy in range(4):
                out_copy(dz, dy).start()

    relay_b()
    for d in (1, 3, 2):
        r_copy(d).wait_recv()

    @pl.when(active)
    def _():
        out_copy(0, 0).wait()

    for dz in range(4):
        @pl.when(head_of(mod(zh - dz, 4)) < HEADS_HERE)
        def _():
            for dy in range(4):
                if dz + dy > 0:
                    out_copy(dz, dy).wait_recv()

    out_proj = jnp.dot(att_buf[...], wo_buf[...], preferred_element_type=jnp.float32)
    out_ref[...] = (x_ref[...].astype(jnp.float32) + mod_ref[2] * out_proj).astype(jnp.bfloat16)

    for i in range(5):
        w_copy(i).wait_send()
        a_copy(i).wait_send()
    for d in (1, 3, 2):
        y_copy(d).wait_send()
        b_copy(d).wait_send()
        r_copy(d).wait_send()

        @pl.when(sends_to(d))
        def _():
            for which in range(3):
                z_copy(which, d).wait_send()

    @pl.when(active)
    def _():
        for d in range(4):
            for i in range(6):
                x_copy(d, i).wait_send()
        for dz in range(4):
            for dy in range(4):
                if dz + dy > 0:
                    out_copy(dz, dy).wait_send()


def body(hidden_states, modulation, w_qkv, w_out, lengths):
    vmem = pl.BlockSpec(memory_space=pltpu.VMEM)
    dma = pltpu.SemaphoreType.DMA
    bf16 = jnp.bfloat16
    updated = pl.pallas_call(
        kernel,
        name="block",
        out_shape=jax.ShapeDtypeStruct((ROWS, WIDTH), bf16),
        in_specs=[pl.BlockSpec(memory_space=pltpu.SMEM)] + [vmem] * 4,
        out_specs=vmem,
        scratch_shapes=[
            pltpu.VMEM((4, ROWS, WIDTH), bf16),
            pltpu.VMEM((3, WIDTH, PART), bf16),
            pltpu.VMEM((WIDTH, WIDTH), bf16),
            pltpu.VMEM((HEADS_HERE, TILE, HD), bf16),
            pltpu.VMEM((HEADS_HERE, TILE, HD), bf16),
            pltpu.VMEM((HEADS_HERE, HD, TILE), bf16),
            pltpu.VMEM((4, TILE, HD), bf16),
            pltpu.VMEM((16, TILE, HD), bf16),
            pltpu.VMEM((16, HD, TILE), bf16),
            pltpu.VMEM((1, 4 * TILE), jnp.float32),
            pltpu.VMEM((1, 4 * TILE), jnp.float32),
            pltpu.VMEM((HD, 4 * TILE), jnp.float32),
            pltpu.VMEM((4 * TILE, HD), bf16),
            pltpu.VMEM((ROWS, WIDTH), bf16),
            dma((5,)), dma((5,)), dma((5,)), dma((5,)),
            dma((4,)), dma((4,)), dma((4,)), dma((4,)), dma((4,)), dma((4,)),
            dma((3, 4)), dma((3, 4)), dma((4, 6)), dma((4, 6)), dma((16,)), dma((16,)), dma((5,)),
        ],
        compiler_params=pltpu.CompilerParams(
            collective_id=0, has_side_effects=True, vmem_limit_bytes=56 << 20
        ),
    )(
        lengths,
        hidden_states[0],
        jnp.transpose(modulation, (1, 0, 2)),
        jnp.transpose(w_qkv, (1, 0, 2)),
        w_out,
    )
    return updated[None]


def solution(mesh):
    placed = (
        P("wrow", ("patch", "wcol"), None),
        P("wrow", None, None),
        P("wrow", None, "wcol"),
        P("wcol", "wrow"),
        P("wrow"),
    )
    return jax.shard_map(
        body,
        mesh=mesh,
        in_specs=placed,
        out_specs=P("wrow", ("patch", "wcol"), None),
        check_vma=False,
    )
```

time: 492 us -> 109 us (0.22)
  waiting for transfers between devices: 311 us -> 0 us
  Pallas kernels: 0 us -> 106 us
  matrix products: 76 us -> 0 us
  local copies, waits for them, and re-layouts: 45.7 us -> 1.77 us
  other arithmetic: 43.1 us -> 0 us
  between operations: 13.6 us -> 0.66 us
    all_gather x5 -> x0, waiting for transfers between devices: 283 us -> none  [the longest x1 105 us: body(): value_piece = lax.all_gather(values, 'patch', axis=1, tiled=True)]
    pallas_call x0 -> x1, Pallas kernels: none -> 106 us  [body(): pl.pallas_call(kernel, name='block', out_shape=jax.ShapeDtypeStruct((ROWS...]
    dot_general x34 -> x0, matrix products: 76 us -> none  [the longest x16 54.9 us: absorb(): jnp.einsum('vhqk,vkhd->vhqd', probs.astype(jnp.bfloat16), value_heads, pr...]
    dynamic_slice x16 -> x0, local copies, waits for them, and re-layouts: 30.6 us -> none  [one_block(): value_block = lax.dynamic_slice_in_dim(value_piece, offset, block_len, 1)]
    reduce_scatter x1 -> x0, waiting for transfers between devices: 27 us -> none  [body(): lax.psum_scatter(partial_out.astype(jnp.bfloat16), 'wcol', scatter_dimens...]
    convert_element_type x19 -> x0, other arithmetic: 24.6 us -> none  [the longest x16 19.9 us: absorb(): probs = jnp.exp(scores - new_peak[..., None]) * valid.astype(jnp.float32)]
    reduce_sum x18 -> x0, other arithmetic: 16.6 us -> none  [the longest x16 14.2 us: absorb(): weight_sum = weight_sum * factor + jnp.sum(probs, axis=-1)]
    while x177 -> x0, local copies, waits for them, and re-layouts: 10.9 us -> none
  transfers between devices with their start and end apart: 6 -> 0, of which waited for: 5 -> 0; matrix products, arithmetic and copies ran while one was open for 28% -> 0% of each run, Pallas kernels for 0% -> 0%
where the time goes in v2:
time: 109 us
  Pallas kernels  106 us (97%)
  local copies, waits for them, and re-layouts  1.77 us (2%)
    pallas_call x1, Pallas kernels, body(): pl.pallas_call(kernel, name='block', out_shape=jax.ShapeDtypeStruct((ROWS...  106 us

profile of v2, /device:TPU:2, one launch (start us, length us, event | category | flops | bytes accessed | tf_op | source)
XLA Modules:
  0.0 108.5 jit_solution(8665418206982618419)
XLA Ops:
  0.7 106.1 %block.1 = bf16[128,1536]{1,0:T(8,128)(2,1)} custom-call(s32[1]{0:T(128)S(6)} %copy.7.len_ref, bf16[128,1536]{1,0:T(8,128)(2,1)} %bitcast.6, f32[3,1,1536]{2,1,0:T(1,128)} %bitcast.7, bf16[3,384,384]{2,1,0:T(8,128)(2,1)} %bitcast.5, bf16[384,384]{1,0:T(8,128)(2,1)} %wo_ref.1), custom_call_target="tpu_custom_call" | custom-call | tf_op jit(solution)/shard_map/block/pallas_call | solution.py:351
  106.8 1.8 %copy.8 = bf16[1,128,1536]{2,1,0:T(8,128)(2,1)} copy(bf16[1,128,1536]{2,1,0:T(8,128)(2,1)} %bitcast.4) | data formatting | bytes 786432

commit v3 on v2

--- a/solution.py
+++ b/solution.py
@@ -19,6 +19,10 @@
 SCORE_SCALE = HD**-0.5 * math.log2(math.e)
 MESH = pl.DeviceIdType.MESH
 
+SLOTS = (0, 1, 3, 2)
+HALF_ROWS = ROWS // 2
+SPAN = (slice(0, 3 * ROWS), slice(3 * ROWS, 4 * ROWS))
+
 ORDER = (
     (0, 0), (0, 1), (0, 3), (1, 0), (0, 2), (3, 0), (1, 1), (1, 3),
     (2, 0), (3, 1), (3, 3), (1, 2), (2, 1), (2, 3), (3, 2), (2, 2),
@@ -47,9 +51,9 @@
 def kernel(
     len_ref, x_ref, mod_ref, w_ref, wo_ref, out_ref,
     rows, weights, wo_buf, q_in, k_in, vt_in,
-    q_buf, k_buf, vt_buf, peak_ref, sum_ref, numer_ref, done_buf, att_buf,
+    rq_buf, rk_buf, rv_buf, q_buf, k_buf, vt_buf, peak_ref, sum_ref, numer_ref, done_buf, att_buf,
     w_send, w_recv, a_send, a_recv, b_send, b_recv, r_send, r_recv, y_send, y_recv,
-    z_send, z_recv, x_send, x_recv, o_send, o_recv, own_sem,
+    h_send, h_recv, z_send, z_recv, x_send, x_recv, o_send, o_recv, own_sem,
 ):
     patch, video, y = lax.axis_index("patch"), lax.axis_index("wrow"), lax.axis_index("wcol")
     zh, x = patch // 4, lax.rem(patch, 4)
@@ -107,15 +111,18 @@
         return remote(part, part, r_send.at[d], r_recv.at[d], partner)
 
     def own_w():
-        return pltpu.make_async_copy(w_ref, weights.at[:, pl.ds(mine_first, PART)], own_sem.at[3])
+        return pltpu.make_async_copy(w_ref, weights.at[:, pl.ds(mine_first, PART)], own_sem.at[6])
 
     def own_wo():
         return pltpu.make_async_copy(
-            wo_ref, wo_buf.at[pl.ds(wo_rows, PART), pl.ds(mine_first, PART)], own_sem.at[4]
+            wo_ref, wo_buf.at[pl.ds(wo_rows, PART), pl.ds(mine_first, PART)], own_sem.at[7]
         )
 
-    def y_copy(d):
-        return remote(rows.at[y], rows.at[y], y_send.at[d], y_recv.at[d], at(dy=d))
+    def y_copy(i):
+        src = rows.at[0] if i < 2 else rows.at[i - 1, pl.ds((i - 2) * HALF_ROWS, HALF_ROWS)]
+        dst = rows.at[1 + i] if i < 2 else rows.at[3, pl.ds((i - 2) * HALF_ROWS, HALF_ROWS)]
+        target = at(dy=1) if i in (0, 2) else at(dy=-1)
+        return remote(src, dst, y_send.at[i], y_recv.at[i], target)
 
     for i in (0, 1, 2):
         w_copy(i).start()
@@ -127,107 +134,190 @@
     values = values - center
     spread = jnp.mean(jnp.square(values), axis=-1, keepdims=True)
     normed = values * lax.rsqrt(spread + EPSILON) * (1.0 + mod_ref[1]) + mod_ref[0]
-    rows[y] = normed.astype(jnp.bfloat16)
-    for d in (1, 3, 2):
-        y_copy(d).start()
-
-    own_wo().wait()
+    rows[0] = normed.astype(jnp.bfloat16)
+    for i in (0, 1):
+        y_copy(i).start()
+
     for i in (0, 1):
         w_copy(i).wait_recv()
         w_copy(3 + i).start()
-    for i in (0, 1, 2):
-        a_copy(i).start()
+    for i in (0, 1):
+        y_copy(i).wait_recv()
+        y_copy(2 + i).start()
     own_w().wait()
     for i in (2, 3, 4):
         w_copy(i).wait_recv()
-    for d in (1, 3, 2):
-        y_copy(d).wait_recv()
+
+    idle = lax.rem(video, 2) * 2 + video // 2
 
     def head_of(row):
-        return mod(row - video - 1, 4)
+        return mod(row - idle - 1, 4)
 
     head = head_of(zh)
     active = head < HEADS_HERE
     head = jnp.minimum(head, HEADS_HERE - 1)
     own_block = zh * 4 + x
-    z_refs = ((q_in, q_buf, zh), (k_in, k_buf, own_block), (vt_in, vt_buf, own_block))
-
-    def z_copy(which, d):
-        source, dest, index = z_refs[which]
+
+    def cut(ref, which, g):
+        return ref.at[:, SPAN[g]] if which == 2 else ref.at[SPAN[g]]
+
+    z_in, z_buf = (q_in, k_in, vt_in), (q_buf, k_buf, vt_buf)
+    turn = 1 - 2 * core
+
+    def takes(d):
+        return head_of(mod(zh + d, 4)) < HEADS_HERE
+
+    def tile_index(which, row):
+        return row if which == 0 else row * 4 + x
+
+    def z_copy(which, g, d):
         there = jnp.minimum(head_of(mod(zh + d, 4)), HEADS_HERE - 1)
         return remote(
-            source.at[there], dest.at[index], z_send.at[which, d], z_recv.at[which, d], at(dzh=d)
+            cut(z_in[which].at[there], which, g),
+            cut(z_buf[which].at[tile_index(which, zh)], which, g),
+            z_send.at[which * 2 + g, d],
+            z_recv.at[which * 2 + g, d],
+            at(dzh=d),
         )
 
-    def sends_to(d):
-        return head_of(mod(zh + d, 4)) < HEADS_HERE
-
-    def own_copy(which):
-        source, dest, index = z_refs[which]
-        return pltpu.make_async_copy(source.at[head], dest.at[index], own_sem.at[which])
-
-    def hand_out(which):
+    def way(which):
+        return -turn if which == 2 else turn
+
+    def first_hop(which, g):
+        there = jnp.minimum(head_of(mod(zh + 2, 4)), HEADS_HERE - 1)
+        return remote(
+            cut(z_in[which].at[there], which, g),
+            cut((rq_buf, rk_buf, rv_buf)[which], which, g),
+            h_send.at[which * 2 + g],
+            h_recv.at[which * 2 + g],
+            at(dzh=way(which)),
+        )
+
+    def second_hop(which, g):
+        source = mod(zh - way(which), 4)
+        return remote(
+            cut((rq_buf, rk_buf, rv_buf)[which], which, g),
+            cut(z_buf[which].at[tile_index(which, source)], which, g),
+            z_send.at[which * 2 + g, 2],
+            z_recv.at[which * 2 + g, 2],
+            at(dzh=way(which)),
+        )
+
+    def own_copy(which, g):
+        return pltpu.make_async_copy(
+            cut(z_in[which].at[head], which, g),
+            cut(z_buf[which].at[tile_index(which, zh)], which, g),
+            own_sem.at[which * 2 + g],
+        )
+
+    def x_copy(d, g, i):
+        source = mod(zh - d, 4)
+        column = (x, x, x, x, mod(x - 1, 4), mod(x + 1, 4))[i]
+        which = 1 + i % 2
+        target = (right, right, left, left, right, left)[i]
+        block = source * 4 + column
+        dst = cut(z_buf[which].at[block], which, g)
+        src = cut(z_in[which].at[head], which, g) if d == 0 and i < 4 else dst
+        return remote(src, dst, x_send.at[d * 2 + g, i], x_recv.at[d * 2 + g, i], target)
+
+    def spread_out(d, g):
+        for i in range(4):
+            x_copy(d, g, i).start()
+
+    def project(g, first, count):
+        flat = rows[pl.ds(first, count)].reshape(count * ROWS, WIDTH)
+        for which in range(3):
+            part = jnp.dot(flat, weights[which], preferred_element_type=jnp.float32)
+            if which == 0:
+                part = part * SCORE_SCALE
+            for h in range(HEADS_HERE):
+                one = part[:, h * HD : (h + 1) * HD]
+                if which == 2:
+                    vt_in[h, :, SPAN[g]] = one.T.astype(jnp.bfloat16)
+                else:
+                    z_in[which][h, SPAN[g]] = one.astype(jnp.bfloat16)
+
+            @pl.when(takes(2))
+            def _():
+                first_hop(which, g).start()
+
+            for d in (1, 3):
+                @pl.when(takes(d))
+                def _():
+                    z_copy(which, g, d).start()
+
+            @pl.when(active)
+            def _():
+                own_copy(which, g).start()
+
         @pl.when(active)
         def _():
-            own_copy(which).start()
-
-        for d in (1, 3, 2):
-            @pl.when(sends_to(d))
+            spread_out(0, g)
+
+    def relay(g):
+        for which in range(3):
+            @pl.when(head_of(mod(zh + way(which), 4)) < HEADS_HERE)
             def _():
-                z_copy(which, d).start()
-
-    flat = rows[...].reshape(4 * ROWS, WIDTH)
-    for which in range(3):
-        part = jnp.dot(flat, weights[which], preferred_element_type=jnp.float32)
-        if which == 0:
-            part = part * SCORE_SCALE
-        for h in range(HEADS_HERE):
-            one = part[:, h * HD : (h + 1) * HD]
-            if which == 2:
-                vt_in[h] = one.T.astype(jnp.bfloat16)
-            else:
-                z_refs[which][0][h] = one.astype(jnp.bfloat16)
-        hand_out(which)
+                first_hop(which, g).wait_recv()
+                second_hop(which, g).start()
+
+    def wait_z(d, g):
+        z_copy(1, g, d).wait_recv()
+        z_copy(2, g, d).wait_recv()
+
+    project(0, 0, 3)
+    for i in (2, 3):
+        y_copy(i).wait_recv()
+    project(1, 3, 1)
+    own_wo().wait()
+    for i in (0, 1, 2):
+        a_copy(i).start()
+    relay(0)
+
+    @pl.when(active)
+    def _():
+        for d in (1, 3):
+            wait_z(d, 0)
+            spread_out(d, 0)
+
+    relay(1)
+
+    @pl.when(active)
+    def _():
+        for d in (1, 3):
+            wait_z(d, 1)
+            spread_out(d, 1)
 
     for i in (0, 1):
         a_copy(i).wait_recv()
         a_copy(3 + i).start()
 
-    def x_copy(d, i):
-        source = mod(zh - d, 4)
-        column = (x, x, x, x, mod(x - 1, 4), mod(x + 1, 4))[i]
-        buf = (k_buf, vt_buf, k_buf, vt_buf, k_buf, vt_buf)[i]
-        target = (right, right, left, left, right, left)[i]
-        block = source * 4 + column
-        return remote(buf.at[block], buf.at[block], x_send.at[d, i], x_recv.at[d, i], target)
-
-    def spread_out(d):
-        for i in range(4):
-            x_copy(d, i).start()
-
-    def wait_z(d):
-        z_copy(1, d).wait_recv()
-        z_copy(2, d).wait_recv()
-
     def pass_on(d):
-        for i in range(4):
-            x_copy(d, i).wait_recv()
-        x_copy(d, 4).start()
-        x_copy(d, 5).start()
+        for g in range(2):
+            for i in range(4):
+                x_copy(d, g, i).wait_recv()
+            x_copy(d, g, 4).start()
+            x_copy(d, g, 5).start()
 
     def wait_far(d):
-        x_copy(d, 4).wait_recv()
-        x_copy(d, 5).wait_recv()
-
-    def out_copy(dz, dy):
-        first = pl.multiple_of(mod(zh + dz, 4) * TILE + mod(y + dy, 4) * ROWS, ROWS)
+        for g in range(2):
+            x_copy(d, g, 4).wait_recv()
+            x_copy(d, g, 5).wait_recv()
+
+    def last_row():
+        for g in range(2):
+            wait_z(2, g)
+            spread_out(2, g)
+
+    def out_copy(dz, slot):
+        first = pl.multiple_of(mod(zh + dz, 4) * TILE + slot * ROWS, ROWS)
         column = pl.multiple_of((y * HEADS_HERE + head) * HD, HD)
-        i = dz * 4 + dy
+        i = dz * 4 + slot
         src = done_buf.at[pl.ds(first, ROWS)]
         dst = att_buf.at[:, pl.ds(column, HD)]
         if i == 0:
             return pltpu.make_async_copy(src, dst, o_send.at[0])
-        return remote(src, dst, o_send.at[i], o_recv.at[i], at(dzh=dz, dy=dy))
+        return remote(src, dst, o_send.at[i], o_recv.at[i], at(dzh=dz, dy=-SLOTS[slot]))
 
     def start_b():
         for i in (2, 3, 4):
@@ -243,13 +333,15 @@
     @pl.when(active)
     def _():
         for which in range(3):
-            own_copy(which).wait()
-        spread_out(0)
+            for g in range(2):
+                own_copy(which, g).wait()
         peak_ref[...] = jnp.full_like(peak_ref, FLOOR)
         sum_ref[...] = jnp.zeros_like(sum_ref)
         numer_ref[...] = jnp.zeros_like(numer_ref)
+        pass_on(0)
         for d in (1, 3, 2):
-            z_copy(0, d).wait_recv()
+            for g in range(2):
+                z_copy(0, g, d).wait_recv()
 
     start_b()
 
@@ -257,15 +349,11 @@
     def _():
         def step(i, carry):
             before = {
-                1: lambda: pass_on(0),
-                3: lambda: (wait_z(1), spread_out(1)),
+                3: last_row,
                 4: lambda: wait_far(0),
-                5: lambda: (wait_z(3), spread_out(3)),
                 6: lambda: pass_on(1),
-                8: lambda: (wait_z(2), spread_out(2)),
-                9: lambda: pass_on(3),
-                11: lambda: wait_far(1),
-                12: lambda: pass_on(2),
+                8: lambda: pass_on(3),
+                11: lambda: (pass_on(2), wait_far(1)),
                 14: lambda: wait_far(3),
                 15: lambda: wait_far(2),
             }
@@ -282,7 +370,11 @@
             scores = lax.dot_general(
                 k_buf[block], queries, (((1,), (1,)), ((), ())), preferred_element_type=jnp.float32
             )
-            position = block * TILE + lax.broadcasted_iota(jnp.int32, (TILE, 1), 0)
+            row = lax.broadcasted_iota(jnp.int32, (TILE, 1), 0)
+            back_y = jnp.zeros_like(row)
+            for slot, dy in enumerate(SLOTS):
+                back_y = jnp.where(row >= slot * ROWS, dy, back_y)
+            position = block * TILE + mod(y - back_y, 4) * ROWS + lax.rem(row, ROWS)
             scores = scores + jnp.where(position < limit, 0.0, FLOOR)
             peak = peak_ref[...]
             new_peak = jnp.maximum(peak, jnp.max(scores, axis=0, keepdims=True))
@@ -298,9 +390,9 @@
         lax.fori_loop(0, 16, step, 0)
         attended = numer_ref[...] / sum_ref[...]
         done_buf[...] = attended.T.astype(jnp.bfloat16)
-        for dz in range(4):
-            for dy in range(4):
-                out_copy(dz, dy).start()
+        for dz in (2, 1, 3, 0):
+            for slot in (3, 1, 2, 0):
+                out_copy(dz, slot).start()
 
     relay_b()
     for d in (1, 3, 2):
@@ -313,9 +405,9 @@
     for dz in range(4):
         @pl.when(head_of(mod(zh - dz, 4)) < HEADS_HERE)
         def _():
-            for dy in range(4):
-                if dz + dy > 0:
-                    out_copy(dz, dy).wait_recv()
+            for slot in range(4):
+                if dz + slot > 0:
+                    out_copy(dz, slot).wait_recv()
 
     out_proj = jnp.dot(att_buf[...], wo_buf[...], preferred_element_type=jnp.float32)
     out_ref[...] = (x_ref[...].astype(jnp.float32) + mod_ref[2] * out_proj).astype(jnp.bfloat16)
@@ -323,25 +415,36 @@
     for i in range(5):
         w_copy(i).wait_send()
         a_copy(i).wait_send()
+    for i in range(4):
+        y_copy(i).wait_send()
     for d in (1, 3, 2):
-        y_copy(d).wait_send()
         b_copy(d).wait_send()
         r_copy(d).wait_send()
-
-        @pl.when(sends_to(d))
-        def _():
-            for which in range(3):
-                z_copy(which, d).wait_send()
+    for which in range(3):
+        for g in range(2):
+            for d in (1, 3):
+                @pl.when(takes(d))
+                def _():
+                    z_copy(which, g, d).wait_send()
+
+            @pl.when(takes(2))
+            def _():
+                first_hop(which, g).wait_send()
+
+            @pl.when(head_of(mod(zh + way(which), 4)) < HEADS_HERE)
+            def _():
+                second_hop(which, g).wait_send()
 
     @pl.when(active)
     def _():
         for d in range(4):
-            for i in range(6):
-                x_copy(d, i).wait_send()
+            for g in range(2):
+                for i in range(6):
+                    x_copy(d, g, i).wait_send()
         for dz in range(4):
-            for dy in range(4):
-                if dz + dy > 0:
-                    out_copy(dz, dy).wait_send()
+            for slot in range(4):
+                if dz + slot > 0:
+                    out_copy(dz, slot).wait_send()
 
 
 def body(hidden_states, modulation, w_qkv, w_out, lengths):
@@ -361,6 +464,9 @@
             pltpu.VMEM((HEADS_HERE, TILE, HD), bf16),
             pltpu.VMEM((HEADS_HERE, TILE, HD), bf16),
             pltpu.VMEM((HEADS_HERE, HD, TILE), bf16),
+            pltpu.VMEM((TILE, HD), bf16),
+            pltpu.VMEM((TILE, HD), bf16),
+            pltpu.VMEM((HD, TILE), bf16),
             pltpu.VMEM((4, TILE, HD), bf16),
             pltpu.VMEM((16, TILE, HD), bf16),
             pltpu.VMEM((16, HD, TILE), bf16),
@@ -371,7 +477,7 @@
             pltpu.VMEM((ROWS, WIDTH), bf16),
             dma((5,)), dma((5,)), dma((5,)), dma((5,)),
             dma((4,)), dma((4,)), dma((4,)), dma((4,)), dma((4,)), dma((4,)),
-            dma((3, 4)), dma((3, 4)), dma((4, 6)), dma((4, 6)), dma((16,)), dma((16,)), dma((5,)),
+            dma((6,)), dma((6,)), dma((6, 4)), dma((6, 4)), dma((8, 6)), dma((8, 6)), dma((16,)), dma((16,)), dma((8,)),
         ],
         compiler_params=pltpu.CompilerParams(
             collective_id=0, has_side_effects=True, vmem_limit_bytes=56 << 20

time: 109 us -> 102 us (0.936)
  Pallas kernels: 106 us -> 99.6 us
    pallas_call x1, Pallas kernels: 106 us -> 99.6 us  [body(): pl.pallas_call(kernel, name='block', out_shape=jax.ShapeDtypeStruct((ROWS...]
where the time goes in v3:
time: 102 us
  Pallas kernels  99.6 us (98%)
  local copies, waits for them, and re-layouts  1.77 us (2%)
    pallas_call x1, Pallas kernels, body(): pl.pallas_call(kernel, name='block', out_shape=jax.ShapeDtypeStruct((ROWS...  99.6 us

profile of v3, /device:TPU:2, one launch (start us, length us, event | category | flops | bytes accessed | tf_op | source)
XLA Modules:
  0.0 102.0 jit_solution(2730206454039508731)
XLA Ops:
  0.7 99.6 %block.1 = bf16[128,1536]{1,0:T(8,128)(2,1)} custom-call(s32[1]{0:T(128)S(6)} %copy.7.len_ref, bf16[128,1536]{1,0:T(8,128)(2,1)} %bitcast.6, f32[3,1,1536]{2,1,0:T(1,128)} %bitcast.7, bf16[3,384,384]{2,1,0:T(8,128)(2,1)} %bitcast.5, bf16[384,384]{1,0:T(8,128)(2,1)} %wo_ref.1), custom_call_target="tpu_custom_call" | custom-call | tf_op jit(solution)/shard_map/block/pallas_call | solution.py:454
  100.3 1.8 %copy.8 = bf16[1,128,1536]{2,1,0:T(8,128)(2,1)} copy(bf16[1,128,1536]{2,1,0:T(8,128)(2,1)} %bitcast.4) | data formatting | bytes 786432

commit v4 on v3

--- a/solution.py
+++ b/solution.py
@@ -21,11 +21,12 @@
 
 SLOTS = (0, 1, 3, 2)
 HALF_ROWS = ROWS // 2
+LAST = 3
 SPAN = (slice(0, 3 * ROWS), slice(3 * ROWS, 4 * ROWS))
 
 ORDER = (
-    (0, 0), (0, 1), (0, 3), (1, 0), (0, 2), (3, 0), (1, 1), (1, 3),
-    (2, 0), (3, 1), (3, 3), (1, 2), (2, 1), (2, 3), (3, 2), (2, 2),
+    (1, 0), (3, 0), (2, 0), (1, 1), (1, 3), (3, 1),
+    (3, 3), (1, 2), (3, 2), (2, 1), (2, 3), (2, 2),
 )
 
 
@@ -280,18 +281,6 @@
             wait_z(d, 0)
             spread_out(d, 0)
 
-    relay(1)
-
-    @pl.when(active)
-    def _():
-        for d in (1, 3):
-            wait_z(d, 1)
-            spread_out(d, 1)
-
-    for i in (0, 1):
-        a_copy(i).wait_recv()
-        a_copy(3 + i).start()
-
     def pass_on(d):
         for g in range(2):
             for i in range(4):
@@ -303,6 +292,22 @@
         for g in range(2):
             x_copy(d, g, 4).wait_recv()
             x_copy(d, g, 5).wait_recv()
+
+    @pl.when(active)
+    def _():
+        pass_on(0)
+
+    relay(1)
+
+    @pl.when(active)
+    def _():
+        for d in (1, 3):
+            wait_z(d, 1)
+            spread_out(d, 1)
+
+    for i in (0, 1):
+        a_copy(i).wait_recv()
+        a_copy(3 + i).start()
 
     def last_row():
         for g in range(2):
@@ -338,59 +343,99 @@
         peak_ref[...] = jnp.full_like(peak_ref, FLOOR)
         sum_ref[...] = jnp.zeros_like(sum_ref)
         numer_ref[...] = jnp.zeros_like(numer_ref)
-        pass_on(0)
-        for d in (1, 3, 2):
-            for g in range(2):
-                z_copy(0, g, d).wait_recv()
 
     start_b()
 
     @pl.when(active)
     def _():
-        def step(i, carry):
-            before = {
-                3: last_row,
-                4: lambda: wait_far(0),
-                6: lambda: pass_on(1),
-                8: lambda: pass_on(3),
-                11: lambda: (pass_on(2), wait_far(1)),
-                14: lambda: wait_far(3),
-                15: lambda: wait_far(2),
-            }
-            for when, act in before.items():
-                @pl.when(i == when)
-                def _():
-                    act()
-            back_z, back_x = 0, 0
-            for when, (dz, dx) in enumerate(ORDER):
-                back_z = jnp.where(i == when, dz, back_z)
-                back_x = jnp.where(i == when, dx, back_x)
-            block = mod(zh - back_z, 4) * 4 + mod(x - back_x, 4)
-            queries = q_buf[...].reshape(4 * TILE, HD)
-            scores = lax.dot_general(
-                k_buf[block], queries, (((1,), (1,)), ((), ())), preferred_element_type=jnp.float32
-            )
+        def block_at(back_z, back_x):
+            return mod(zh - back_z, 4) * 4 + mod(x - back_x, 4)
+
+        def bias(block):
             row = lax.broadcasted_iota(jnp.int32, (TILE, 1), 0)
             back_y = jnp.zeros_like(row)
             for slot, dy in enumerate(SLOTS):
                 back_y = jnp.where(row >= slot * ROWS, dy, back_y)
             position = block * TILE + mod(y - back_y, 4) * ROWS + lax.rem(row, ROWS)
-            scores = scores + jnp.where(position < limit, 0.0, FLOOR)
-            peak = peak_ref[...]
-            new_peak = jnp.maximum(peak, jnp.max(scores, axis=0, keepdims=True))
+            return jnp.where(position < limit, 0.0, FLOOR)
+
+        def absorb(blocks, queries, peak, total, numer):
+            scores = []
+            for block in blocks:
+                one = lax.dot_general(
+                    k_buf[block], queries, (((1,), (1,)), ((), ())), preferred_element_type=jnp.float32
+                )
+                scores.append(one + bias(block))
+            new_peak = peak
+            for one in scores:
+                new_peak = jnp.maximum(new_peak, jnp.max(one, axis=0, keepdims=True))
             factor = jnp.exp2(peak - new_peak)
-            probs = jnp.exp2(scores - new_peak).astype(jnp.bfloat16)
-            with_ones = jnp.concatenate([vt_buf[block], jnp.ones((16, TILE), jnp.bfloat16)], 0)
-            mixed = jnp.dot(with_ones, probs, preferred_element_type=jnp.float32)
-            peak_ref[...] = new_peak
-            sum_ref[...] = sum_ref[...] * factor + mixed[HD : HD + 1]
-            numer_ref[...] = numer_ref[...] * factor + mixed[:HD]
+            total, numer = total * factor, numer * factor
+            for block, one in zip(blocks, scores):
+                probs = jnp.exp2(one - new_peak).astype(jnp.bfloat16)
+                with_ones = jnp.concatenate([vt_buf[block], jnp.ones((16, TILE), jnp.bfloat16)], 0)
+                mixed = jnp.dot(with_ones, probs, preferred_element_type=jnp.float32)
+                total, numer = total + mixed[HD : HD + 1], numer + mixed[:HD]
+            return new_peak, total, numer
+
+        wait_far(0)
+        near_blocks = [block_at(0, dx) for dx in (0, 1, 3, 2)]
+
+        def own_row(i, carry):
+            for when, d in ((1, 1), (2, 3), (3, 2)):
+                @pl.when(i == when)
+                def _():
+                    if d == 2:
+                        last_row()
+                    for g in range(2):
+                        z_copy(0, g, d).wait_recv()
+            back = jnp.where(i == 1, 1, jnp.where(i == 2, 3, jnp.where(i == 3, 2, 0)))
+            tile = mod(zh - back, 4)
+            columns = pl.ds(pl.multiple_of(tile * TILE, TILE), TILE)
+            peak_ref[:, columns], sum_ref[:, columns], numer_ref[:, columns] = absorb(
+                near_blocks, q_buf[tile], peak_ref[:, columns], sum_ref[:, columns], numer_ref[:, columns]
+            )
             return carry
 
-        lax.fori_loop(0, 16, step, 0)
-        attended = numer_ref[...] / sum_ref[...]
-        done_buf[...] = attended.T.astype(jnp.bfloat16)
+        lax.fori_loop(0, 4, own_row, 0)
+        before = {
+            1: lambda: pass_on(1),
+            2: lambda: pass_on(3),
+            4: lambda: pass_on(2),
+            7: lambda: wait_far(1),
+            8: lambda: wait_far(3),
+            9: lambda: wait_far(2),
+        }
+
+        def step(i, carry):
+            for when, act in before.items():
+                if when < 12 - LAST:
+                    @pl.when(i == when)
+                    def _():
+                        act()
+            back_z, back_x = 0, 0
+            for when, (dz, dx) in enumerate(ORDER):
+                back_z = jnp.where(i == when, dz, back_z)
+                back_x = jnp.where(i == when, dx, back_x)
+            queries = q_buf[...].reshape(4 * TILE, HD)
+            peak_ref[...], sum_ref[...], numer_ref[...] = absorb(
+                [block_at(back_z, back_x)], queries, peak_ref[...], sum_ref[...], numer_ref[...]
+            )
+            return carry
+
+        lax.fori_loop(0, 12 - LAST, step, 0)
+        for when, act in before.items():
+            if when >= 12 - LAST:
+                act()
+
+        blocks = [block_at(*back) for back in ORDER[12 - LAST :]]
         for dz in (2, 1, 3, 0):
+            tile = mod(zh + dz, 4)
+            columns = pl.ds(pl.multiple_of(tile * TILE, TILE), TILE)
+            _, total, numer = absorb(
+                blocks, q_buf[tile], peak_ref[:, columns], sum_ref[:, columns], numer_ref[:, columns]
+            )
+            done_buf[columns] = (numer / total).T.astype(jnp.bfloat16)
             for slot in (3, 1, 2, 0):
                 out_copy(dz, slot).start()
 

time: 102 us -> 99.8 us (0.978); the launches traced: 102 us -> 98.4 us
  Pallas kernels: 99.6 us -> 96 us
    pallas_call x1, Pallas kernels: 99.6 us -> 96 us  [body(): pl.pallas_call(kernel, name='block', out_shape=jax.ShapeDtypeStruct((ROWS...]
where the time goes in v4:
time: 99.8 us; the launch traced here: 98.4 us
  Pallas kernels  96 us (96%)
  local copies, waits for them, and re-layouts  1.77 us (2%)
    pallas_call x1, Pallas kernels, body(): pl.pallas_call(kernel, name='block', out_shape=jax.ShapeDtypeStruct((ROWS...  96 us

profile of v4, /device:TPU:2, one launch (start us, length us, event | category | flops | bytes accessed | tf_op | source)
XLA Modules:
  0.0 98.4 jit_solution(1363851294512687072)
XLA Ops:
  0.7 96.0 %block.1 = bf16[128,1536]{1,0:T(8,128)(2,1)} custom-call(s32[1]{0:T(128)S(6)} %copy.7.len_ref, bf16[128,1536]{1,0:T(8,128)(2,1)} %bitcast.6, f32[3,1,1536]{2,1,0:T(1,128)} %bitcast.7, bf16[3,384,384]{2,1,0:T(8,128)(2,1)} %bitcast.5, bf16[384,384]{1,0:T(8,128)(2,1)} %wo_ref.1), custom_call_target="tpu_custom_call" | custom-call | tf_op jit(solution)/shard_map/block/pallas_call | solution.py:499
  96.6 1.8 %copy.8 = bf16[1,128,1536]{2,1,0:T(8,128)(2,1)} copy(bf16[1,128,1536]{2,1,0:T(8,128)(2,1)} %bitcast.4) | data formatting | bytes 786432

commit v5 on v4

--- a/solution.py
+++ b/solution.py
@@ -385,7 +385,7 @@
             for when, d in ((1, 1), (2, 3), (3, 2)):
                 @pl.when(i == when)
                 def _():
-                    if d == 2:
+                    if d == 3:
                         last_row()
                     for g in range(2):
                         z_copy(0, g, d).wait_recv()
@@ -399,9 +399,9 @@
 
         lax.fori_loop(0, 4, own_row, 0)
         before = {
-            1: lambda: pass_on(1),
-            2: lambda: pass_on(3),
-            4: lambda: pass_on(2),
+            0: lambda: pass_on(1),
+            1: lambda: pass_on(3),
+            3: lambda: pass_on(2),
             7: lambda: wait_far(1),
             8: lambda: wait_far(3),
             9: lambda: wait_far(2),

time: 99.8 us -> 99.8 us (level)
  no operation moved by 1% of the time
where the time goes in v5:
time: 99.8 us; the launch traced here: 98.4 us
  Pallas kernels  96 us (96%)
  local copies, waits for them, and re-layouts  1.77 us (2%)
    pallas_call x1, Pallas kernels, body(): pl.pallas_call(kernel, name='block', out_shape=jax.ShapeDtypeStruct((ROWS...  96 us

profile of v5, /device:TPU:2, one launch (start us, length us, event | category | flops | bytes accessed | tf_op | source)
XLA Modules:
  0.0 98.4 jit_solution(9754653908449335969)
XLA Ops:
  0.7 96.0 %block.1 = bf16[128,1536]{1,0:T(8,128)(2,1)} custom-call(s32[1]{0:T(128)S(6)} %copy.7.len_ref, bf16[128,1536]{1,0:T(8,128)(2,1)} %bitcast.6, f32[3,1,1536]{2,1,0:T(1,128)} %bitcast.7, bf16[3,384,384]{2,1,0:T(8,128)(2,1)} %bitcast.5, bf16[384,384]{1,0:T(8,128)(2,1)} %wo_ref.1), custom_call_target="tpu_custom_call" | custom-call | tf_op jit(solution)/shard_map/block/pallas_call | solution.py:499
  96.6 1.8 %copy.8 = bf16[1,128,1536]{2,1,0:T(8,128)(2,1)} copy(bf16[1,128,1536]{2,1,0:T(8,128)(2,1)} %bitcast.4) | data formatting | bytes 786432
